TPU v7x, 32 devices: a whole 2x2x4 slice. The times are simulated.
32 devices in a mesh: dp: 8 (over z, core), space: 4 (over y, x).
Axes of the slice: x: 2, y: 2, z: 4, core: 2. Of those that a mesh axis runs over, the one named last changes fastest.
Arguments:
- volume: bfloat16 [8, 8, 32, 32, 128], P('dp', 'space'), may hold values from -6 to 6
- filter_one: bfloat16 [3, 3, 3, 128, 128], replicated, may hold values from -0.109375 to 0.109375
- filter_two: bfloat16 [3, 3, 3, 128, 128], replicated, may hold values from -0.109375 to 0.109375
- cotangent: bfloat16 [8, 8, 32, 32, 128], P('dp', 'space'), may hold values from -6 to 6
Outputs:
- block_out: bfloat16 [8, 8, 32, 32, 128], P('dp', 'space')
- input_grad: bfloat16 [8, 8, 32, 32, 128], P('dp', 'space')
- grad_one: float32 [3, 3, 3, 128, 128], replicated
- grad_two: float32 [3, 3, 3, 128, 128], replicated
All inputs are finite; a program needn't handle non-finite values.
Results may differ from a plain program's by a relative error of at most 0.0031.
Values may be sent and summed in bfloat16 or wider, within the bound.
No kernel may reach another device: no remote copies, remote signals or barrier semaphores. Data moves between devices by JAX's collectives and lax.ppermute only.
A program may use at most 128 MiB of HBM per device.

v0:
```python
import functools
import math

import jax
import jax.numpy as jnp
from jax import lax
from jax.experimental import pallas as pl
from jax.experimental.pallas import tpu as pltpu
from jax.sharding import PartitionSpec as P

AXES = ("dp", "space")
LIMIT = 20 * 2**20
VMEM = pl.BlockSpec(memory_space=pltpu.VMEM)
SMEM = pl.BlockSpec(memory_space=pltpu.SMEM)
ANY = pl.BlockSpec(memory_space=pl.ANY)
BF16, F32 = jnp.bfloat16, jnp.float32


def divisor(n, most):
    return max(d for d in range(1, most + 1) if n % d == 0)


def factors(n):
    out = []
    while n > 1:
        f = 4 if n % 4 == 0 else 2
        out.append(f)
        n //= f
    return out


def swap_to(value, stride, size, offset, devices):
    def partner(rank):
        digit = (rank // stride) % size
        return rank + ((digit ^ offset) - digit) * stride

    return lax.ppermute(value, AXES, [(rank, partner(rank)) for rank in range(devices)])


def call(kernel, outs, args, scalars=(), order=(), scratch=(), flops=0, name=None):
    size = sum(a.size * a.dtype.itemsize for a in args) + sum(o.size * o.dtype.itemsize for o in outs)
    used = len(scalars) + len(args)

    def body(*refs):
        kernel(*refs[:used], *refs[used + len(order) :])

    return pl.pallas_call(
        body,
        out_shape=list(outs),
        in_specs=[SMEM] * len(scalars) + [VMEM] * len(args) + [ANY] * len(order),
        out_specs=[VMEM] * len(outs),
        scratch_shapes=list(scratch),
        cost_estimate=pl.CostEstimate(flops=flops, bytes_accessed=size, transcendentals=0),
        compiler_params=pltpu.CompilerParams(vmem_limit_bytes=LIMIT),
        name=name,
    )(*[s.reshape(1) for s in scalars], *args, *order)


def blocks(count, most, body):
    step = divisor(count, most)

    def one(i, carry):
        body(pl.multiple_of(i * step, step), step)
        return carry

    lax.fori_loop(0, count // step, one, 0)


def copy(source, target):
    target[...] = source[...]


def tiles(count, chans, dtype):
    return jax.ShapeDtypeStruct((count, 8, chans), dtype)


def join_kernel(size, pairs, digit_ref, *refs):
    given, rest = refs[: 2 * pairs], refs[2 * pairs :]
    part = given[0].shape[0] // size
    digit = digit_ref[0]
    for offset in range(size):
        target = rest[offset]
        for pair in range(pairs):
            kept, got = given[2 * pair], given[2 * pair + 1]

            def move(at, step, kept=kept, got=got, target=target, pair=pair, offset=offset):
                here = pl.ds((digit ^ offset) * part + at, step)
                value = kept[here] + got[here].astype(F32)
                target[pl.ds(pair * part + at, step)] = value.astype(target.dtype)

            blocks(part, 32, move)
        spare = target.shape[0] - pairs * part
        if spare:
            target[pl.ds(pairs * part, spare)] = jnp.zeros((spare,) + target.shape[1:], target.dtype)


def scatter_kernel(size, arrived, carried, digit_ref, *refs):
    kept, got = refs[0], refs[1 : 1 + arrived]
    moved = refs[1 + arrived : 1 + arrived + carried]
    outs = refs[1 + arrived + carried :]
    for source, target in zip(moved, outs[size:]):
        copy(source, target)
    digit = digit_ref[0]
    piece = outs[0].shape[0]
    for offset in range(size):
        base = (digit ^ offset) * piece if size > 1 else 0

        def move(at, step, base=base, target=outs[offset]):
            value = kept[pl.ds(base + at, step)]
            for other in got:
                value = value + other[pl.ds(base + at, step)].astype(F32)
            target[pl.ds(at, step)] = value.astype(target.dtype)

        blocks(piece, 32, move)


def gather_kernel(size, digit_ref, *refs):
    out = refs[size]
    digit = digit_ref[0]
    piece = refs[0].shape[0]
    for offset in range(size):
        base = (digit ^ offset) * piece

        def move(at, step, base=base, source=refs[offset]):
            out[pl.ds(base + at, step)] = source[pl.ds(at, step)]

        blocks(piece, 32, move)


def finish_kernel(size, part, factor, core_ref, digit_ref, *refs):
    outs = refs[2 * size :]
    half = size * part
    for side in range(2):
        core = core_ref[0] ^ side
        for offset in range(size):
            source = refs[side * size + offset]
            for i, out in enumerate(outs):

                def move(at, step, source=source, out=out, core=core, offset=offset, i=i):
                    to = core * half + (digit_ref[0] ^ offset) * part + at
                    out[pl.ds(to, step)] = source[pl.ds(i * part + at, step)].astype(F32) * factor

                blocks(part, 32, move)


def turn_kernel(one_ref, two_ref, one_out, two_out):
    for source, target in ((one_ref, one_out), (two_ref, two_out)):
        chans = source.shape[1]
        taps = source.shape[0] // chans

        def turn(tap, carry, source=source, target=target, taps=taps, chans=chans):
            block = source[pl.ds(pl.multiple_of((taps - 1 - tap) * chans, chans), chans), :]
            to = pl.ds(pl.multiple_of(tap * chans, chans), chans)
            target[to, :] = jnp.transpose(block.astype(F32)).astype(BF16)
            return carry

        lax.fori_loop(0, taps, turn, 0, unroll=3)


def spread(source, plane, wide, slot, side):
    chans = source.shape[-1]
    step = 8 * side
    edge = jnp.zeros((side, 3 * chans), BF16)
    wide[slot, pl.ds(0, side), :] = edge
    wide[slot, pl.ds(side + source.shape[1], side), :] = edge
    column = lax.broadcasted_iota(jnp.int32, (step, chans), 0) % side

    def some(i, carry):
        at = pl.multiple_of(i * step, step)
        value = source[plane, pl.ds(at, step), :]
        full = value.astype(F32)
        left = jnp.where(column == 0, 0.0, pltpu.roll(full, 1, 0))
        right = jnp.where(column == side - 1, 0.0, pltpu.roll(full, step - 1, 0))
        to = pl.ds(pl.multiple_of(at + side, side), step)
        wide[slot, to, pl.ds(0, chans)] = left.astype(BF16)
        wide[slot, to, pl.ds(chans, chans)] = value
        wide[slot, to, pl.ds(2 * chans, chans)] = right.astype(BF16)
        return carry

    lax.fori_loop(0, source.shape[1] // step, some, 0)


def spread_all(own, low, high, wide, side):
    planes = own.shape[0]
    spread(low, 0, wide, 0, side)
    for plane in range(planes):
        spread(own, plane, wide, plane + 1, side)
    spread(high, 0, wide, planes + 1, side)


def conv(wide, weights, side, finish):
    slots, rows = wide.shape[0], wide.shape[1] - 2 * side
    planes, chans = slots - 2, weights.shape[1]
    depth = 9 * chans
    step = STEP * side
    empty = jnp.zeros((depth, chans), BF16)

    def some(i, carry):
        at = pl.multiple_of(i * step, step)
        left = jnp.concatenate(
            [
                wide[slot, pl.ds(pl.multiple_of(at + dy * side, side), step), :]
                for slot in range(slots)
                for dy in range(3)
            ],
            axis=-1,
        )
        right = jnp.concatenate(
            [
                jnp.concatenate(
                    [
                        weights[pl.ds((slot - out) * depth, depth), :] if 0 <= slot - out <= 2 else empty
                        for out in range(planes)
                    ],
                    axis=-1,
                )
                for slot in range(slots)
            ],
            axis=0,
        )
        sums = jnp.dot(left, right, preferred_element_type=F32)
        for plane in range(planes):
            finish(plane, pl.ds(at, step), sums[:, plane * chans : (plane + 1) * chans])
        return carry

    lax.fori_loop(0, rows // step, some, 0)


def silu_kernel(side, own, low, high, weights, wide, act, first, last, slope):
    spread_all(own, low, high, wide, side)

    def finish(plane, at, pre):
        sigma = 1.0 / (1.0 + jnp.exp(-pre))
        value = (pre * sigma).astype(BF16)
        act[plane, at, :] = value
        if plane == 0:
            first[0, at, :] = value
        if plane == own.shape[0] - 1:
            last[0, at, :] = value
        slope[plane, at, :] = sigma * (1.0 + pre * (1.0 - sigma))

    conv(wide, weights, side, finish)


def slope_kernel(side, own, low, high, weights, slope, wide, grad):
    spread_all(own, low, high, wide, side)

    def finish(plane, at, part):
        grad[plane, at, :] = (part * slope[plane, at, :]).astype(BF16)

    conv(wide, weights, side, finish)


def add_kernel(side, own, low, high, weights, base, out, wide):
    spread_all(own, low, high, wide, side)

    def finish(plane, at, part):
        out[plane, at, :] = (base[plane, at, :].astype(F32) + part).astype(BF16)

    conv(wide, weights, side, finish)


def outer_kernel(turned, core_ref, own, wide, keep, send, flat, sums, full):
    planes, rows, chans = own.shape
    side = (wide.shape[1] - rows) // 2
    for plane in range(planes):
        for i in range(rows // 256):
            value = own[plane, pl.ds(i * 256, 256), :].astype(F32)
            flat[pl.ds(plane * chans, chans), pl.ds(i * 256, 256)] = jnp.transpose(value).astype(BF16)
    for slot in range(planes + 2):
        begin, end = max(0, slot - 2), min(planes, slot + 1)
        right = jnp.concatenate([wide[slot, pl.ds(dy * side, rows), :] for dy in range(3)], axis=-1)
        left = flat[pl.ds(begin * chans, (end - begin) * chans), :]
        product = jnp.dot(left, right, preferred_element_type=F32)
        for plane in range(begin, end):
            part = product[(plane - begin) * chans : (plane - begin + 1) * chans]
            sums[slot - plane] = part if plane == 0 else sums[slot - plane] + part
    deep = chans // 8
    for kz in range(3):
        for tap in range(9):
            part = sums[kz, :, pl.ds(tap * chans, chans)]
            index = kz * 9 + tap if turned else 26 - kz * 9 - tap
            part = jnp.transpose(part) if turned else part
            full[pl.ds(index * deep, deep)] = part.reshape(deep, 8, chans)
    half = keep.shape[0]
    for target, core in ((keep, core_ref[0]), (send, 1 - core_ref[0])):

        def move(at, step, target=target, core=core):
            target[pl.ds(at, step)] = full[pl.ds(core * half + at, step)].astype(target.dtype)

        blocks(half, 32, move)


def edge_kernel(cells, first, last):
    first[0] = cells[0]
    last[0] = cells[cells.shape[0] - 1]


def from_sides(first, last):
    count = lax.axis_size("space")
    low = lax.ppermute(last, "space", [(i, i + 1) for i in range(count - 1)])
    high = lax.ppermute(first, "space", [(i + 1, i) for i in range(count - 1)])
    return low, high


STEP = 32


def local(volume, filter_one, filter_two, cotangent):
    _, planes, side, _, chans = volume.shape
    rows = side * side
    dp, space = lax.axis_size("dp"), lax.axis_size("space")
    devices = dp * space
    rank = lax.axis_index("dp") * space + lax.axis_index("space")
    core = (rank // space) % 2
    field = volume.reshape(planes, rows, chans)
    grad_out = cotangent.reshape(planes, rows, chans)
    w_one = filter_one.reshape(-1, chans)
    w_two = filter_two.reshape(-1, chans)
    slab = jax.ShapeDtypeStruct((planes, rows, chans), BF16)
    plane = jax.ShapeDtypeStruct((1, rows, chans), BF16)
    wide = jax.ShapeDtypeStruct((planes + 2, rows + 2 * side, 3 * chans), BF16)
    flops = 2 * planes * rows * 27 * chans * chans
    half = 27 * chans // 16

    stages, stride = [], 1
    for size in factors(space):
        stages.append((stride, size))
        stride *= size
    stride = 2 * space
    for size in factors(dp // 2):
        stages.append((stride, size))
        stride *= size
    digits = [(rank // stride) % size for stride, size in stages]

    x_edges = call(edge_kernel, [plane] * 2, [field], name="edges_x")
    low_x, high_x = from_sides(*x_edges)
    back_one, back_two = call(
        turn_kernel,
        [jax.ShapeDtypeStruct(w_one.shape, BF16)] * 2,
        [w_one, w_two],
        order=x_edges,
        name="turn",
    )
    g_edges = call(edge_kernel, [plane] * 2, [grad_out], order=[back_two], name="edges_g")
    low_g, high_g = from_sides(*g_edges)
    wide_x, act, act_first, act_last, slope = call(
        functools.partial(silu_kernel, side),
        [wide, slab, plane, plane, jax.ShapeDtypeStruct(slab.shape, F32)],
        [field, low_x, high_x, w_one],
        flops=flops,
        name="conv_pre",
    )
    low_a, high_a = from_sides(act_first, act_last)
    wide_g, grad_pre = call(
        functools.partial(slope_kernel, side),
        [wide, slab],
        [grad_out, low_g, high_g, back_two, slope],
        flops=flops,
        name="conv_act_grad",
    )

    def outer(turned, own, spread_out, order, name):
        return call(
            functools.partial(outer_kernel, turned),
            [tiles(half, chans, F32)] * 2,
            [own, spread_out],
            scalars=[core],
            order=order,
            scratch=[
                pltpu.VMEM((planes * chans, rows), BF16),
                pltpu.VMEM((3, chans, 9 * chans), F32),
                pltpu.VMEM((2 * half, 8, chans), F32),
            ],
            flops=flops,
            name=name,
        )

    keep_two, send_two = outer(False, act, wide_g, [], "outer_two")
    got_two = swap_to(send_two, space, 2, 1, devices)
    keep_one, send_one = outer(True, grad_pre, wide_x, [send_two], "outer_one")
    got_one = swap_to(send_one, space, 2, 1, devices)

    def conv_out(order):
        return call(
            functools.partial(add_kernel, side),
            [slab],
            [act, low_a, high_a, w_two, field],
            order=order,
            scratch=[pltpu.VMEM(wide.shape, BF16)],
            flops=flops,
            name="conv_out",
        )[0]

    def conv_in(order, low_d, high_d):
        return call(
            functools.partial(add_kernel, side),
            [slab],
            [grad_pre, low_d, high_d, back_one, grad_out],
            order=order,
            scratch=[pltpu.VMEM(wide.shape, BF16)],
            flops=flops,
            name="conv_in",
        )[0]

    (stride, size), digit = stages[0], digits[0]
    rest = devices // 2 // size
    piece = -(-2 * half // size // rest) * rest
    kept, *sends = call(
        functools.partial(join_kernel, size, 2),
        [tiles(piece, chans, F32)] + [tiles(piece, chans, BF16)] * (size - 1),
        [keep_two, got_two, keep_one, got_one],
        scalars=[digit],
        name="join",
    )
    got = [swap_to(s, stride, size, i + 1, devices) for i, s in enumerate(sends)]
    order = [conv_out([kept])]
    block_out = order[0]
    d_edges = None
    for (stride, size), digit in zip(stages[1:], digits[1:]):
        piece = kept.shape[0] // size
        carried = [] if d_edges else [grad_pre[:1], grad_pre[planes - 1 :]]
        outs = call(
            functools.partial(scatter_kernel, size, len(got), len(carried)),
            [tiles(piece, chans, F32)] + [tiles(piece, chans, BF16)] * (size - 1) + [plane] * len(carried),
            [kept, *got, *carried],
            scalars=[digit],
            order=order,
            name="scatter",
        )
        kept, sends = outs[0], outs[1:size]
        got = [swap_to(s, stride, size, i + 1, devices) for i, s in enumerate(sends)]
        if carried:
            d_edges = from_sides(*outs[size:])
        order = []
    (mine,) = call(
        functools.partial(scatter_kernel, 1, len(got), 0),
        [tiles(kept.shape[0], chans, BF16)],
        [kept, *got],
        scalars=[digits[0]],
        name="sum",
    )
    input_grad = conv_in([mine], *d_edges)
    order = [input_grad]
    for (stride, size), digit in list(zip(stages, digits))[:0:-1]:
        pieces = [mine] + [swap_to(mine, stride, size, o, devices) for o in range(1, size)]
        (mine,) = call(
            functools.partial(gather_kernel, size),
            [tiles(size * mine.shape[0], chans, BF16)],
            pieces,
            scalars=[digit],
            order=order,
            name="gather",
        )
        order = []
    (stride, size), digit = stages[0], digits[0]
    pieces = [mine] + [swap_to(mine, stride, size, o, devices) for o in range(1, size)]
    others = [swap_to(p, space, 2, 1, devices) for p in pieces]
    factor = 1.0 / math.sqrt(devices * planes * rows)
    grad_one, grad_two = call(
        functools.partial(finish_kernel, size, half // size, factor),
        [tiles(2 * half, chans, F32)] * 2,
        pieces + others,
        scalars=[core, digit],
        name="finish",
    )[::-1]
    shape = filter_one.shape
    return (
        block_out.reshape(volume.shape),
        input_grad.reshape(volume.shape),
        grad_one.reshape(shape),
        grad_two.reshape(shape),
    )


def solution(mesh):
    cells, whole = P("dp", "space", None, None, None), P()
    return jax.shard_map(
        local,
        mesh=mesh,
        in_specs=(cells, whole, whole, cells),
        out_specs=(cells, cells, whole, whole),
        check_vma=False,
    )
```

profile of v0, /device:TPU:0, one launch (start us, length us, event | category | flops | bytes accessed | tf_op | source)
XLA Modules:
  0.0 110.7 jit_solution(9710416283533157317)
XLA Ops:
  1.7 5.0 %collective-permute-start = (bf16[1,1024,128]{2,1,0:T(8,128)(2,1)S(1)}, bf16[1,1024,128]{2,1,0:T(8,128)(2,1)S(1)}, u32[]{:S(2)}, u32[]{:S(2)}) collective-permute-start(bf16[1,1024,128]{2,1,0:T(8,128)(2,1)S(1)} %get-tuple-element.33.refs_3_), channel_id=1, source_target_pairs={{0,1},{1,2},{2,3},{4,5},{5,6},{6,7},{8,9},{9,10},{10,11},{12,13},{... | collective-permute-start | bytes 786440 | tf_op jit(solution)/shard_map/ppermute | solution.py:301
  10.4 2.0 %turn.1 = (bf16[3456,128]{1,0:T(8,128)(2,1)S(1)}, bf16[3456,128]{1,0:T(8,128)(2,1)S(1)}) custom-call(bf16[3456,128]{1,0:T(8,128)(2,1)S(1)} %bitcast.11, bf16[3456,128]{1,0:T(8,128)(2,1)S(1)} %bitcast.13, bf16[1,1024,128]{2,1,0:T(8,128)(2,1)S(1)} %get-tuple-element.34.refs_2_, bf16[1,1024,128]{2,1,0:T(8,128)(2,1)S(1)} %get-tuple-element.33.refs_3_), custom_call_target="tpu_custom_call" | custom-call | bytes 3538944 | tf_op jit(solution)/shard_map/turn/pallas_call | solution.py:47
  14.6 4.6 %collective-permute-start.4 = (bf16[1,1024,128]{2,1,0:T(8,128)(2,1)}, bf16[1,1024,128]{2,1,0:T(8,128)(2,1)S(1)}, u32[]{:S(2)}, u32[]{:S(2)}) collective-permute-start(bf16[1,1024,128]{2,1,0:T(8,128)(2,1)} %get-tuple-element.39), channel_id=1, source_target_pairs={{0,1},{1,2},{2,3},{4,5},{5,6},{6,7},{8,9},{9,10},{10,11},{12,13},{... | collective-permute-start | bytes 786440 | tf_op jit(solution)/shard_map/ppermute | solution.py:301
  20.5 5.3 %conv_pre.1 = (bf16[4,1088,384]{2,1,0:T(8,128)(2,1)S(1)}, bf16[2,1024,128]{2,1,0:T(8,128)(2,1)S(1)}, bf16[1,1024,128]{2,1,0:T(8,128)(2,1)}, bf16[1,1024,128]{2,1,0:T(8,128)(2,1)}, f32[2,1024,128]{2,1,0:T(8,128)S(1)}) custom-call(bf16[2,1024,128]{2,1,0:T(8,128)(2,1)S(1)} %bitcast.18, bf16[1,1024,128]{2,1,0:T(8,128)(2,1)S(1)} %collective-permute-done.refs_1_, ...), custom_call_target="tpu_custom_call" | custom-call | flops 1811939328 | bytes 7372800 | tf_op jit(solution)/shard_map/conv_pre/pallas_call | solution.py:47
  25.8 7.0 %collective-permute-done.5.refs_2_ = bf16[1,1024,128]{2,1,0:T(8,128)(2,1)} collective-permute-done((bf16[1,1024,128]{2,1,0:T(8,128)(2,1)}, bf16[1,1024,128]{2,1,0:T(8,128)(2,1)}, u32[]{:S(2)}, u32[]{:S(2)}) %collective-permute-start.5) | collective-permute-done | bytes 262176 | tf_op jit(solution)/shard_map/ppermute | solution.py:302
  32.9 4.3 %conv_act_grad.1 = (bf16[4,1088,384]{2,1,0:T(8,128)(2,1)S(1)}, bf16[2,1024,128]{2,1,0:T(8,128)(2,1)S(1)}) custom-call(bf16[2,1024,128]{2,1,0:T(8,128)(2,1)S(1)} %bitcast.21, bf16[1,1024,128]{2,1,0:T(8,128)(2,1)S(1)} %collective-permute-done.4.refs_1_, bf16[1,1024,128]{2,1,0:T(8,128)(2,1)} %collective-permute-done.5.refs_2_, ...), custom_call_target="tpu_custom_call" | custom-call | flops 1811939328 | bytes 6848512 | tf_op jit(solution)/shard_map/conv_act_grad/pallas_call | solution.py:47
  37.2 3.3 %outer_two.1 = (f32[216,8,128]{2,1,0:T(8,128)S(1)}, f32[216,8,128]{2,1,0:T(8,128)}) custom-call(s32[1]{0:T(128)} %bitcast.4.refs_0_, bf16[2,1024,128]{2,1,0:T(8,128)(2,1)S(1)} %get-tuple-element.35.refs_1_.refs_0_, bf16[4,1088,384]{2,1,0:T(8,128)(2,1)S(1)} %get-tuple-element.42.refs_2_), custom_call_target="tpu_custom_call" | custom-call | flops 1811939328 | bytes 5636096 | tf_op jit(solution)/shard_map/outer_two/pallas_call | solution.py:47
  40.6 3.4 %outer_one.1 = (f32[216,8,128]{2,1,0:T(8,128)S(1)}, f32[216,8,128]{2,1,0:T(8,128)}) custom-call(s32[1]{0:T(128)} %bitcast.4.refs_0_, bf16[2,1024,128]{2,1,0:T(8,128)(2,1)S(1)} %get-tuple-element.45.refs_1_.refs_0_, bf16[4,1088,384]{2,1,0:T(8,128)(2,1)S(1)} %get-tuple-element.46.refs_2_, f32[216,8,128]{2,1,0:T(8,128)} %get-tuple-element.44.refs_3_), custom_call_target="tpu_custom_call" | custom-call | flops 1811939328 | bytes 5636096 | tf_op jit(solution)/shard_map/outer_one/pallas_call | solution.py:47
  44.5 3.9 %collective-permute-start.2 = (bf16[1,1024,128]{2,1,0:T(8,128)(2,1)}, bf16[1,1024,128]{2,1,0:T(8,128)(2,1)}, u32[]{:S(2)}, u32[]{:S(2)}) collective-permute-start(bf16[1,1024,128]{2,1,0:T(8,128)(2,1)} %get-tuple-element.36), channel_id=1, source_target_pairs={{0,1},{1,2},{2,3},{4,5},{5,6},{6,7},{8,9},{9,10},{10,11},{12,13},{... | collective-permute-start | bytes 786440 | tf_op jit(solution)/shard_map/ppermute | solution.py:301
  51.3 2.7 %collective-permute-start.8 = (bf16[108,8,128]{2,1,0:T(8,128)(2,1)S(1)}, bf16[108,8,128]{2,1,0:T(8,128)(2,1)S(1)}, u32[]{:S(2)}, u32[]{:S(2)}) collective-permute-start(bf16[108,8,128]{2,1,0:T(8,128)(2,1)S(1)} %get-tuple-element.50), channel_id=1, source_target_pairs={{0,1},{1,0},{2,3},{3,2},{4,5},{5,4},{6,7},{7,6},{8,9},{9,8},{10,11... | collective-permute-start | bytes 663560 | tf_op jit(solution)/shard_map/ppermute | solution.py:37
  55.6 5.2 %collective-permute-done.3.refs_2_ = bf16[1,1024,128]{2,1,0:T(8,128)(2,1)} collective-permute-done((bf16[1,1024,128]{2,1,0:T(8,128)(2,1)}, bf16[1,1024,128]{2,1,0:T(8,128)(2,1)}, u32[]{:S(2)}, u32[]{:S(2)}) %collective-permute-start.3) | collective-permute-done | bytes 262176 | tf_op jit(solution)/shard_map/ppermute | solution.py:302
  60.8 5.3 %conv_out.1.refs_7_ = bf16[2,1024,128]{2,1,0:T(8,128)(2,1)} custom-call(bf16[2,1024,128]{2,1,0:T(8,128)(2,1)S(1)} %copy-done.17, bf16[1,1024,128]{2,1,0:T(8,128)(2,1)} %collective-permute-done.2.refs_1_, bf16[1,1024,128]{2,1,0:T(8,128)(2,1)} %collective-permute-done.3.refs_2_, bf16[3456,128]{1,0:T(8,128)(2,1)S(1)} %bitcast.14, ...), custom_call_target="tpu_custom_call" | custom-call | flops 1811939328 | bytes 2981888 | tf_op jit(solution)/shard_map/conv_out/pallas_call | solution.py:47
  67.3 4.8 %collective-permute-start.11 = (bf16[1,1024,128]{2,1,0:T(8,128)(2,1)S(1)}, bf16[1,1024,128]{2,1,0:T(8,128)(2,1)S(1)}, u32[]{:S(2)}, u32[]{:S(2)}) collective-permute-start(bf16[1,1024,128]{2,1,0:T(8,128)(2,1)S(1)} %get-tuple-element.53), channel_id=1, source_target_pairs={{0,1},{1,2},{2,3},{4,5},{5,6},{6,7},{8,9},{9,10},{10,11},{12,13},{... | collective-permute-start | bytes 786440 | tf_op jit(solution)/shard_map/ppermute | solution.py:301
  73.7 1.6 %collective-permute-start.13 = (bf16[27,8,128]{2,1,0:T(8,128)(2,1)S(1)}, bf16[27,8,128]{2,1,0:T(8,128)(2,1)S(1)}, u32[]{:S(2)}, u32[]{:S(2)}) collective-permute-start(bf16[27,8,128]{2,1,0:T(8,128)(2,1)S(1)} %get-tuple-element.57), channel_id=1, source_target_pairs={{0,8},{1,9},{2,10},{3,11},{4,12},{5,13},{6,14},{7,15},{8,0},{9,1},... | collective-permute-start | bytes 165896 | tf_op jit(solution)/shard_map/ppermute | solution.py:37
  75.3 2.6 %collective-permute-start.14 = (bf16[27,8,128]{2,1,0:T(8,128)(2,1)S(1)}, bf16[27,8,128]{2,1,0:T(8,128)(2,1)S(1)}, u32[]{:S(2)}, u32[]{:S(2)}) collective-permute-start(bf16[27,8,128]{2,1,0:T(8,128)(2,1)S(1)} %get-tuple-element.58), channel_id=1, source_target_pairs={{0,16},{1,17},{2,18},{3,19},{4,20},{5,21},{6,22},{7,23},{8,24},{9,... | collective-permute-start | bytes 165896 | tf_op jit(solution)/shard_map/ppermute | solution.py:37
  78.4 2.6 %collective-permute-done.14.refs_3_ = bf16[27,8,128]{2,1,0:T(8,128)(2,1)S(1)} collective-permute-done((bf16[27,8,128]{2,1,0:T(8,128)(2,1)S(1)}, bf16[27,8,128]{2,1,0:T(8,128)(2,1)S(1)}, u32[]{:S(2)}, u32[]{:S(2)}) %collective-permute-start.14) | collective-permute-done | bytes 55328 | tf_op jit(solution)/shard_map/ppermute | solution.py:37
  80.9 2.9 %collective-permute-done.15.refs_4_ = bf16[27,8,128]{2,1,0:T(8,128)(2,1)S(1)} collective-permute-done((bf16[27,8,128]{2,1,0:T(8,128)(2,1)S(1)}, bf16[27,8,128]{2,1,0:T(8,128)(2,1)S(1)}, u32[]{:S(2)}, u32[]{:S(2)}) %collective-permute-start.15) | collective-permute-done | bytes 55328 | tf_op jit(solution)/shard_map/ppermute | solution.py:37
  84.6 3.7 %collective-permute-start.16 = (bf16[27,8,128]{2,1,0:T(8,128)(2,1)S(1)}, bf16[27,8,128]{2,1,0:T(8,128)(2,1)S(1)}, u32[]{:S(2)}, u32[]{:S(2)}) collective-permute-start(bf16[27,8,128]{2,1,0:T(8,128)(2,1)S(1)} %sum.1.refs_5_.refs_1_), channel_id=1, source_target_pairs={{0,8},{1,9},{2,10},{3,11},{4,12},{5,13},{6,14},{7,15},{8,0},{9,1},... | collective-permute-start | bytes 165896 | tf_op jit(solution)/shard_map/ppermute | solution.py:37
  88.3 4.2 %conv_in.1.refs_5_ = bf16[2,1024,128]{2,1,0:T(8,128)(2,1)} custom-call(bf16[2,1024,128]{2,1,0:T(8,128)(2,1)S(1)} %copy-done.10, bf16[1,1024,128]{2,1,0:T(8,128)(2,1)S(1)} %collective-permute-done.11.refs_1_, bf16[1,1024,128]{2,1,0:T(8,128)(2,1)S(1)} %collective-permute-done.12.refs_2_, bf16[3456,128]{1,0:T(8,128)(2,1)S(1)} %copy-done.15, ...), custom_call_target="tpu_custom_call" | custom-call | flops 1811939328 | bytes 2981888 | tf_op jit(solution)/shard_map/conv_in/pallas_call | solution.py:47
  93.6 4.0 %collective-permute-start.21 = (bf16[108,8,128]{2,1,0:T(8,128)(2,1)S(1)}, bf16[108,8,128]{2,1,0:T(8,128)(2,1)S(1)}, u32[]{:S(2)}, u32[]{:S(2)}) collective-permute-start(bf16[108,8,128]{2,1,0:T(8,128)(2,1)S(1)} %gather.1.refs_2_), channel_id=1, source_target_pairs={{0,3},{1,2},{2,1},{3,0},{4,7},{5,6},{6,5},{7,4},{8,11},{9,10},{10,... | collective-permute-start | bytes 663560 | tf_op jit(solution)/shard_map/ppermute | solution.py:37
  100.5 2.9 %collective-permute-done.21.refs_5_ = bf16[108,8,128]{2,1,0:T(8,128)(2,1)S(1)} collective-permute-done((bf16[108,8,128]{2,1,0:T(8,128)(2,1)S(1)}, bf16[108,8,128]{2,1,0:T(8,128)(2,1)S(1)}, u32[]{:S(2)}, u32[]{:S(2)}) %collective-permute-start.21) | collective-permute-done | bytes 221216 | tf_op jit(solution)/shard_map/ppermute | solution.py:37
  103.5 1.6 %collective-permute-done.20.refs_4_ = bf16[108,8,128]{2,1,0:T(8,128)(2,1)S(1)} collective-permute-done((bf16[108,8,128]{2,1,0:T(8,128)(2,1)S(1)}, bf16[108,8,128]{2,1,0:T(8,128)(2,1)S(1)}, u32[]{:S(2)}, u32[]{:S(2)}) %collective-permute-start.20) | collective-permute-done | bytes 221216 | tf_op jit(solution)/shard_map/ppermute | solution.py:37
  105.1 1.9 %collective-permute-done.19.refs_3_ = bf16[108,8,128]{2,1,0:T(8,128)(2,1)S(1)} collective-permute-done((bf16[108,8,128]{2,1,0:T(8,128)(2,1)S(1)}, bf16[108,8,128]{2,1,0:T(8,128)(2,1)S(1)}, u32[]{:S(2)}, u32[]{:S(2)}) %collective-permute-start.19) | collective-permute-done | bytes 221216 | tf_op jit(solution)/shard_map/ppermute | solution.py:37
  108.5 2.3 %finish.1 = (f32[432,8,128]{2,1,0:T(8,128)}, f32[432,8,128]{2,1,0:T(8,128)}) custom-call(s32[1]{0:T(128)} %bitcast.4.refs_0_, s32[1]{0:T(128)} %bitcast.3.refs_0_.refs_1_, bf16[108,8,128]{2,1,0:T(8,128)(2,1)S(1)} %gather.1.refs_2_, bf16[108,8,128]{2,1,0:T(8,128)(2,1)S(1)} %collective-permute-done.19.refs_3_, ...), custom_call_target="tpu_custom_call" | custom-call | bytes 5308416 | tf_op jit(solution)/shard_map/finish/pallas_call | solution.py:47
  (79 shorter events, 22.5 us)
Async XLA Ops:
  1.7 18.8 %collective-permute-start = (bf16[1,1024,128]{2,1,0:T(8,128)(2,1)S(1)}, bf16[1,1024,128]{2,1,0:T(8,128)(2,1)S(1)}, u32[]{:S(2)}, u32[]{:S(2)}) collective-permute-start(bf16[1,1024,128]{2,1,0:T(8,128)(2,1)S(1)} %get-tuple-element.33.refs_3_), channel_id=1, source_target_pairs={{0,1},{1,2},{2,3},{4,5},{5,6},{6,7},{8,9},{9,10},{10,11},{12,13},{... | collective-permute-start | bytes 786440 | tf_op jit(solution)/shard_map/ppermute | solution.py:301
  6.7 13.8 %collective-permute-start.1 = (bf16[1,1024,128]{2,1,0:T(8,128)(2,1)S(1)}, bf16[1,1024,128]{2,1,0:T(8,128)(2,1)}, u32[]{:S(2)}, u32[]{:S(2)}) collective-permute-start(bf16[1,1024,128]{2,1,0:T(8,128)(2,1)S(1)} %get-tuple-element.34.refs_2_), channel_id=1, source_target_pairs={{1,0},{2,1},{3,2},{5,4},{6,5},{7,6},{9,8},{10,9},{11,10},{13,12},{... | collective-permute-start | bytes 786440 | tf_op jit(solution)/shard_map/ppermute | solution.py:302
  14.6 11.3 %collective-permute-start.4 = (bf16[1,1024,128]{2,1,0:T(8,128)(2,1)}, bf16[1,1024,128]{2,1,0:T(8,128)(2,1)S(1)}, u32[]{:S(2)}, u32[]{:S(2)}) collective-permute-start(bf16[1,1024,128]{2,1,0:T(8,128)(2,1)} %get-tuple-element.39), channel_id=1, source_target_pairs={{0,1},{1,2},{2,3},{4,5},{5,6},{6,7},{8,9},{9,10},{10,11},{12,13},{... | collective-permute-start | bytes 786440 | tf_op jit(solution)/shard_map/ppermute | solution.py:301
  19.1 13.7 %collective-permute-start.5 = (bf16[1,1024,128]{2,1,0:T(8,128)(2,1)}, bf16[1,1024,128]{2,1,0:T(8,128)(2,1)}, u32[]{:S(2)}, u32[]{:S(2)}) collective-permute-start(bf16[1,1024,128]{2,1,0:T(8,128)(2,1)} %get-tuple-element.40), channel_id=1, source_target_pairs={{1,0},{2,1},{3,2},{5,4},{6,5},{7,6},{9,8},{10,9},{11,10},{13,12},{... | collective-permute-start | bytes 786440 | tf_op jit(solution)/shard_map/ppermute | solution.py:302
  44.0 5.8 %collective-permute-start.7 = (f32[216,8,128]{2,1,0:T(8,128)}, f32[216,8,128]{2,1,0:T(8,128)S(1)}, u32[]{:S(2)}, u32[]{:S(2)}) collective-permute-start(f32[216,8,128]{2,1,0:T(8,128)} %get-tuple-element.48), channel_id=1, source_target_pairs={{0,4},{1,5},{2,6},{3,7},{4,0},{5,1},{6,2},{7,3},{8,12},{9,13},{10,... | collective-permute-start | bytes 2654216 | tf_op jit(solution)/shard_map/ppermute | solution.py:37
  44.0 5.8 %collective-permute-start.6 = (f32[216,8,128]{2,1,0:T(8,128)}, f32[216,8,128]{2,1,0:T(8,128)}, u32[]{:S(2)}, u32[]{:S(2)}) collective-permute-start(f32[216,8,128]{2,1,0:T(8,128)} %get-tuple-element.44.refs_3_), channel_id=1, source_target_pairs={{0,4},{1,5},{2,6},{3,7},{4,0},{5,1},{6,2},{7,3},{8,12},{9,13},{10,... | collective-permute-start | bytes 2654216 | tf_op jit(solution)/shard_map/ppermute | solution.py:37
  44.5 11.1 %collective-permute-start.2 = (bf16[1,1024,128]{2,1,0:T(8,128)(2,1)}, bf16[1,1024,128]{2,1,0:T(8,128)(2,1)}, u32[]{:S(2)}, u32[]{:S(2)}) collective-permute-start(bf16[1,1024,128]{2,1,0:T(8,128)(2,1)} %get-tuple-element.36), channel_id=1, source_target_pairs={{0,1},{1,2},{2,3},{4,5},{5,6},{6,7},{8,9},{9,10},{10,11},{12,13},{... | collective-permute-start | bytes 786440 | tf_op jit(solution)/shard_map/ppermute | solution.py:301
  48.4 12.4 %collective-permute-start.3 = (bf16[1,1024,128]{2,1,0:T(8,128)(2,1)}, bf16[1,1024,128]{2,1,0:T(8,128)(2,1)}, u32[]{:S(2)}, u32[]{:S(2)}) collective-permute-start(bf16[1,1024,128]{2,1,0:T(8,128)(2,1)} %get-tuple-element.37), channel_id=1, source_target_pairs={{1,0},{2,1},{3,2},{5,4},{6,5},{7,6},{9,8},{10,9},{11,10},{13,12},{... | collective-permute-start | bytes 786440 | tf_op jit(solution)/shard_map/ppermute | solution.py:302
  51.3 14.8 %collective-permute-start.8 = (bf16[108,8,128]{2,1,0:T(8,128)(2,1)S(1)}, bf16[108,8,128]{2,1,0:T(8,128)(2,1)S(1)}, u32[]{:S(2)}, u32[]{:S(2)}) collective-permute-start(bf16[108,8,128]{2,1,0:T(8,128)(2,1)S(1)} %get-tuple-element.50), channel_id=1, source_target_pairs={{0,1},{1,0},{2,3},{3,2},{4,5},{5,4},{6,7},{7,6},{8,9},{9,8},{10,11... | collective-permute-start | bytes 663560 | tf_op jit(solution)/shard_map/ppermute | solution.py:37
  54.0 12.1 %collective-permute-start.9 = (bf16[108,8,128]{2,1,0:T(8,128)(2,1)S(1)}, bf16[108,8,128]{2,1,0:T(8,128)(2,1)S(1)}, u32[]{:S(2)}, u32[]{:S(2)}) collective-permute-start(bf16[108,8,128]{2,1,0:T(8,128)(2,1)S(1)} %get-tuple-element.51), channel_id=1, source_target_pairs={{0,2},{1,3},{2,0},{3,1},{4,6},{5,7},{6,4},{7,5},{8,10},{9,11},{10,... | collective-permute-start | bytes 663560 | tf_op jit(solution)/shard_map/ppermute | solution.py:37
  54.0 12.1 %collective-permute-start.10 = (bf16[108,8,128]{2,1,0:T(8,128)(2,1)S(1)}, bf16[108,8,128]{2,1,0:T(8,128)(2,1)S(1)}, u32[]{:S(2)}, u32[]{:S(2)}) collective-permute-start(bf16[108,8,128]{2,1,0:T(8,128)(2,1)S(1)} %get-tuple-element.52), channel_id=1, source_target_pairs={{0,3},{1,2},{2,1},{3,0},{4,7},{5,6},{6,5},{7,4},{8,11},{9,10},{10,... | collective-permute-start | bytes 663560 | tf_op jit(solution)/shard_map/ppermute | solution.py:37
  67.3 21.0 %collective-permute-start.11 = (bf16[1,1024,128]{2,1,0:T(8,128)(2,1)S(1)}, bf16[1,1024,128]{2,1,0:T(8,128)(2,1)S(1)}, u32[]{:S(2)}, u32[]{:S(2)}) collective-permute-start(bf16[1,1024,128]{2,1,0:T(8,128)(2,1)S(1)} %get-tuple-element.53), channel_id=1, source_target_pairs={{0,1},{1,2},{2,3},{4,5},{5,6},{6,7},{8,9},{9,10},{10,11},{12,13},{... | collective-permute-start | bytes 786440 | tf_op jit(solution)/shard_map/ppermute | solution.py:301
  72.2 16.2 %collective-permute-start.12 = (bf16[1,1024,128]{2,1,0:T(8,128)(2,1)S(1)}, bf16[1,1024,128]{2,1,0:T(8,128)(2,1)S(1)}, u32[]{:S(2)}, u32[]{:S(2)}) collective-permute-start(bf16[1,1024,128]{2,1,0:T(8,128)(2,1)S(1)} %get-tuple-element.54), channel_id=1, source_target_pairs={{1,0},{2,1},{3,2},{5,4},{6,5},{7,6},{9,8},{10,9},{11,10},{13,12},{... | collective-permute-start | bytes 786440 | tf_op jit(solution)/shard_map/ppermute | solution.py:302
  73.7 4.7 %collective-permute-start.13 = (bf16[27,8,128]{2,1,0:T(8,128)(2,1)S(1)}, bf16[27,8,128]{2,1,0:T(8,128)(2,1)S(1)}, u32[]{:S(2)}, u32[]{:S(2)}) collective-permute-start(bf16[27,8,128]{2,1,0:T(8,128)(2,1)S(1)} %get-tuple-element.57), channel_id=1, source_target_pairs={{0,8},{1,9},{2,10},{3,11},{4,12},{5,13},{6,14},{7,15},{8,0},{9,1},... | collective-permute-start | bytes 165896 | tf_op jit(solution)/shard_map/ppermute | solution.py:37
  75.3 5.6 %collective-permute-start.14 = (bf16[27,8,128]{2,1,0:T(8,128)(2,1)S(1)}, bf16[27,8,128]{2,1,0:T(8,128)(2,1)S(1)}, u32[]{:S(2)}, u32[]{:S(2)}) collective-permute-start(bf16[27,8,128]{2,1,0:T(8,128)(2,1)S(1)} %get-tuple-element.58), channel_id=1, source_target_pairs={{0,16},{1,17},{2,18},{3,19},{4,20},{5,21},{6,22},{7,23},{8,24},{9,... | collective-permute-start | bytes 165896 | tf_op jit(solution)/shard_map/ppermute | solution.py:37
  77.9 6.0 %collective-permute-start.15 = (bf16[27,8,128]{2,1,0:T(8,128)(2,1)S(1)}, bf16[27,8,128]{2,1,0:T(8,128)(2,1)S(1)}, u32[]{:S(2)}, u32[]{:S(2)}) collective-permute-start(bf16[27,8,128]{2,1,0:T(8,128)(2,1)S(1)} %get-tuple-element.59), channel_id=1, source_target_pairs={{0,24},{1,25},{2,26},{3,27},{4,28},{5,29},{6,30},{7,31},{8,16},{9,... | collective-permute-start | bytes 165896 | tf_op jit(solution)/shard_map/ppermute | solution.py:37
  83.9 8.6 %collective-permute-start.18 = (bf16[27,8,128]{2,1,0:T(8,128)(2,1)S(1)}, bf16[27,8,128]{2,1,0:T(8,128)(2,1)S(1)}, u32[]{:S(2)}, u32[]{:S(2)}) collective-permute-start(bf16[27,8,128]{2,1,0:T(8,128)(2,1)S(1)} %sum.1.refs_5_.refs_1_), channel_id=1, source_target_pairs={{0,24},{1,25},{2,26},{3,27},{4,28},{5,29},{6,30},{7,31},{8,16},{9,... | collective-permute-start | bytes 165896 | tf_op jit(solution)/shard_map/ppermute | solution.py:37
  84.6 7.9 %collective-permute-start.17 = (bf16[27,8,128]{2,1,0:T(8,128)(2,1)S(1)}, bf16[27,8,128]{2,1,0:T(8,128)(2,1)S(1)}, u32[]{:S(2)}, u32[]{:S(2)}) collective-permute-start(bf16[27,8,128]{2,1,0:T(8,128)(2,1)S(1)} %sum.1.refs_5_.refs_1_), channel_id=1, source_target_pairs={{0,16},{1,17},{2,18},{3,19},{4,20},{5,21},{6,22},{7,23},{8,24},{9,... | collective-permute-start | bytes 165896 | tf_op jit(solution)/shard_map/ppermute | solution.py:37
  84.6 7.9 %collective-permute-start.16 = (bf16[27,8,128]{2,1,0:T(8,128)(2,1)S(1)}, bf16[27,8,128]{2,1,0:T(8,128)(2,1)S(1)}, u32[]{:S(2)}, u32[]{:S(2)}) collective-permute-start(bf16[27,8,128]{2,1,0:T(8,128)(2,1)S(1)} %sum.1.refs_5_.refs_1_), channel_id=1, source_target_pairs={{0,8},{1,9},{2,10},{3,11},{4,12},{5,13},{6,14},{7,15},{8,0},{9,1},... | collective-permute-start | bytes 165896 | tf_op jit(solution)/shard_map/ppermute | solution.py:37
  93.6 9.9 %collective-permute-start.21 = (bf16[108,8,128]{2,1,0:T(8,128)(2,1)S(1)}, bf16[108,8,128]{2,1,0:T(8,128)(2,1)S(1)}, u32[]{:S(2)}, u32[]{:S(2)}) collective-permute-start(bf16[108,8,128]{2,1,0:T(8,128)(2,1)S(1)} %gather.1.refs_2_), channel_id=1, source_target_pairs={{0,3},{1,2},{2,1},{3,0},{4,7},{5,6},{6,5},{7,4},{8,11},{9,10},{10,... | collective-permute-start | bytes 663560 | tf_op jit(solution)/shard_map/ppermute | solution.py:37
  97.6 7.4 %collective-permute-start.20 = (bf16[108,8,128]{2,1,0:T(8,128)(2,1)S(1)}, bf16[108,8,128]{2,1,0:T(8,128)(2,1)S(1)}, u32[]{:S(2)}, u32[]{:S(2)}) collective-permute-start(bf16[108,8,128]{2,1,0:T(8,128)(2,1)S(1)} %gather.1.refs_2_), channel_id=1, source_target_pairs={{0,2},{1,3},{2,0},{3,1},{4,6},{5,7},{6,4},{7,5},{8,10},{9,11},{10,... | collective-permute-start | bytes 663560 | tf_op jit(solution)/shard_map/ppermute | solution.py:37
  99.1 7.9 %collective-permute-start.19 = (bf16[108,8,128]{2,1,0:T(8,128)(2,1)S(1)}, bf16[108,8,128]{2,1,0:T(8,128)(2,1)S(1)}, u32[]{:S(2)}, u32[]{:S(2)}) collective-permute-start(bf16[108,8,128]{2,1,0:T(8,128)(2,1)S(1)} %gather.1.refs_2_), channel_id=1, source_target_pairs={{0,1},{1,0},{2,3},{3,2},{4,5},{5,4},{6,7},{7,6},{8,9},{9,8},{10,11... | collective-permute-start | bytes 663560 | tf_op jit(solution)/shard_map/ppermute | solution.py:37
  100.5 6.5 %collective-permute-start.22 = (bf16[108,8,128]{2,1,0:T(8,128)(2,1)S(1)}, bf16[108,8,128]{2,1,0:T(8,128)(2,1)S(1)}, u32[]{:S(2)}, u32[]{:S(2)}) collective-permute-start(bf16[108,8,128]{2,1,0:T(8,128)(2,1)S(1)} %gather.1.refs_2_), channel_id=1, source_target_pairs={{0,4},{1,5},{2,6},{3,7},{4,0},{5,1},{6,2},{7,3},{8,12},{9,13},{10,... | collective-permute-start | bytes 663560 | tf_op jit(solution)/shard_map/ppermute | solution.py:37
  103.5 3.6 %collective-permute-start.25 = (bf16[108,8,128]{2,1,0:T(8,128)(2,1)S(1)}, bf16[108,8,128]{2,1,0:T(8,128)(2,1)S(1)}, u32[]{:S(2)}, u32[]{:S(2)}) collective-permute-start(bf16[108,8,128]{2,1,0:T(8,128)(2,1)S(1)} %collective-permute-done.21.refs_5_), channel_id=1, source_target_pairs={{0,4},{1,5},{2,6},{3,7},{4,0},{5,1},{6,2},{7,3},{8,12},{9,13},{10,... | collective-permute-start | bytes 663560 | tf_op jit(solution)/shard_map/ppermute | solution.py:37
  (20 other events, 168.4 us)
where the time goes:
time: 111 us
  starting transfers between devices  44.3 us (40%)
  Pallas kernels  32.7 us (29%)
  waiting for transfers between devices  25.9 us (23%)
  local copies, waits for them, and re-layouts  6.89 us (6%)
    pallas_call x14, Pallas kernels, call(): pl.pallas_call(body, out_shape=list(outs), in_specs=[SMEM] * len(scalars)...  32.7 us
    ppermute x18, starting transfers between devices, swap_to(): lax.ppermute(value, AXES, [(rank, partner(rank)) for rank in range(device...  20.6 us
    ppermute x4, starting transfers between devices, from_sides(): low = lax.ppermute(last, 'space', [(i, i + 1) for i in range(count - 1)])  18.3 us
    ppermute x18, waiting for transfers between devices, swap_to(): lax.ppermute(value, AXES, [(rank, partner(rank)) for rank in range(device...  13.7 us
    ppermute x4, waiting for transfers between devices, from_sides(): high = lax.ppermute(first, 'space', [(i + 1, i) for i in range(count - 1)])  12.2 us
    unnamed x36, local copies, waits for them, and re-layouts  6.86 us
    ppermute x4, starting transfers between devices, from_sides(): high = lax.ppermute(first, 'space', [(i + 1, i) for i in range(count - 1)])  5.34 us
  transfers between devices with their start and end apart: 26, of which 9 were waited for; matrix products, arithmetic and copies ran while one was open for 0% of the time, Pallas kernels for 17%

commit v1 on v0

--- a/solution.py
+++ b/solution.py
@@ -11,7 +11,6 @@
 AXES = ("dp", "space")
 LIMIT = 20 * 2**20
 VMEM = pl.BlockSpec(memory_space=pltpu.VMEM)
-SMEM = pl.BlockSpec(memory_space=pltpu.SMEM)
 ANY = pl.BlockSpec(memory_space=pl.ANY)
 BF16, F32 = jnp.bfloat16, jnp.float32
 
@@ -39,21 +38,22 @@
 
 def call(kernel, outs, args, scalars=(), order=(), scratch=(), flops=0, name=None):
     size = sum(a.size * a.dtype.itemsize for a in args) + sum(o.size * o.dtype.itemsize for o in outs)
-    used = len(scalars) + len(args)
+    used = len(args)
 
     def body(*refs):
-        kernel(*refs[:used], *refs[used + len(order) :])
+        rank = lax.axis_index("dp") * lax.axis_size("space") + lax.axis_index("space")
+        kernel(*[[scalar(rank)] for scalar in scalars], *refs[:used], *refs[used + len(order) :])
 
     return pl.pallas_call(
         body,
         out_shape=list(outs),
-        in_specs=[SMEM] * len(scalars) + [VMEM] * len(args) + [ANY] * len(order),
+        in_specs=[VMEM] * len(args) + [ANY] * len(order),
         out_specs=[VMEM] * len(outs),
         scratch_shapes=list(scratch),
         cost_estimate=pl.CostEstimate(flops=flops, bytes_accessed=size, transcendentals=0),
         compiler_params=pltpu.CompilerParams(vmem_limit_bytes=LIMIT),
         name=name,
-    )(*[s.reshape(1) for s in scalars], *args, *order)
+    )(*args, *order)
 
 
 def blocks(count, most, body):
@@ -180,12 +180,12 @@
     lax.fori_loop(0, source.shape[1] // step, some, 0)
 
 
-def spread_all(own, low, high, wide, side):
+def spread_all(odd, own, near, far, wide, side):
     planes = own.shape[0]
-    spread(low, 0, wide, 0, side)
     for plane in range(planes):
         spread(own, plane, wide, plane + 1, side)
-    spread(high, 0, wide, planes + 1, side)
+    spread(near, 0, wide, (planes + 1) * (1 - odd), side)
+    spread(far, 0, wide, (planes + 1) * odd, side)
 
 
 def conv(wide, weights, side, finish):
@@ -226,24 +226,22 @@
     lax.fori_loop(0, rows // step, some, 0)
 
 
-def silu_kernel(side, own, low, high, weights, wide, act, first, last, slope):
-    spread_all(own, low, high, wide, side)
+def silu_kernel(side, odd_ref, own, near, far, weights, wide, act, to_near, to_far, slope):
+    odd = odd_ref[0]
+    spread_all(odd, own, near, far, wide, side)
 
     def finish(plane, at, pre):
         sigma = 1.0 / (1.0 + jnp.exp(-pre))
         value = (pre * sigma).astype(BF16)
         act[plane, at, :] = value
-        if plane == 0:
-            first[0, at, :] = value
-        if plane == own.shape[0] - 1:
-            last[0, at, :] = value
         slope[plane, at, :] = sigma * (1.0 + pre * (1.0 - sigma))
 
     conv(wide, weights, side, finish)
-
-
-def slope_kernel(side, own, low, high, weights, slope, wide, grad):
-    spread_all(own, low, high, wide, side)
+    ends(odd, act, to_near, to_far)
+
+
+def slope_kernel(side, odd_ref, own, near, far, weights, slope, wide, grad):
+    spread_all(odd_ref[0], own, near, far, wide, side)
 
     def finish(plane, at, part):
         grad[plane, at, :] = (part * slope[plane, at, :]).astype(BF16)
@@ -251,8 +249,8 @@
     conv(wide, weights, side, finish)
 
 
-def add_kernel(side, own, low, high, weights, base, out, wide):
-    spread_all(own, low, high, wide, side)
+def add_kernel(side, odd_ref, own, near, far, weights, base, out, wide):
+    spread_all(odd_ref[0], own, near, far, wide, side)
 
     def finish(plane, at, part):
         out[plane, at, :] = (base[plane, at, :].astype(F32) + part).astype(BF16)
@@ -260,9 +258,12 @@
     conv(wide, weights, side, finish)
 
 
-def outer_kernel(turned, core_ref, own, wide, keep, send, flat, sums, full):
+def outer_kernel(turned, core_ref, odd_ref, own, wide, keep, send, *rest):
     planes, rows, chans = own.shape
     side = (wide.shape[1] - rows) // 2
+    flat, sums, full = rest[-3:]
+    if len(rest) > 3:
+        ends(odd_ref[0], own, *rest[:2])
     for plane in range(planes):
         for i in range(rows // 256):
             value = own[plane, pl.ds(i * 256, 256), :].astype(F32)
@@ -291,16 +292,45 @@
         blocks(half, 32, move)
 
 
-def edge_kernel(cells, first, last):
-    first[0] = cells[0]
-    last[0] = cells[cells.shape[0] - 1]
-
-
-def from_sides(first, last):
-    count = lax.axis_size("space")
-    low = lax.ppermute(last, "space", [(i, i + 1) for i in range(count - 1)])
-    high = lax.ppermute(first, "space", [(i + 1, i) for i in range(count - 1)])
-    return low, high
+def ends(odd, cells, to_near, to_far):
+    last = cells.shape[0] - 1
+    to_near[0] = cells[last * (1 - odd)]
+    to_far[0] = cells[last * odd]
+
+
+def edge_kernel(odd_ref, cells, to_near, to_far):
+    ends(odd_ref[0], cells, to_near, to_far)
+
+
+class Places:
+    def __init__(self, dp, space):
+        self.dp, self.space = dp, space
+        self.even = dp % 2 == 0 and space % 2 == 0
+
+    def other(self, rank):
+        sample, slab = rank // self.space, rank % self.space
+        if not self.even:
+            return rank
+        low, bit = sample % 2, slab % 2
+        return (sample - low + bit) * self.space + slab - bit + low
+
+    def move(self, value):
+        pairs = [(rank, self.other(rank)) for rank in range(self.dp * self.space)]
+        return lax.ppermute(value, AXES, pairs)
+
+    def shift(self, value, links):
+        pairs = [
+            (self.other(sample * self.space + a), self.other(sample * self.space + b))
+            for sample in range(self.dp)
+            for i, j in links
+            for a, b in ((i, j), (j, i))
+        ]
+        return lax.ppermute(value, AXES, pairs)
+
+    def sides(self, to_near, to_far):
+        near = self.shift(to_near, [(i, i + 1) for i in range(0, self.space - 1, 2)])
+        far = self.shift(to_far, [(i, i + 1) for i in range(1, self.space - 1, 2)])
+        return near, far
 
 
 STEP = 32
@@ -311,10 +341,13 @@
     rows = side * side
     dp, space = lax.axis_size("dp"), lax.axis_size("space")
     devices = dp * space
-    rank = lax.axis_index("dp") * space + lax.axis_index("space")
-    core = (rank // space) % 2
-    field = volume.reshape(planes, rows, chans)
-    grad_out = cotangent.reshape(planes, rows, chans)
+
+    def digit_of(stride, size):
+        return lambda rank: (rank // stride) % size
+
+    core = digit_of(space, 2)
+    places = Places(dp, space)
+    odd = core if places.even else digit_of(1, 2)
     w_one = filter_one.reshape(-1, chans)
     w_two = filter_two.reshape(-1, chans)
     slab = jax.ShapeDtypeStruct((planes, rows, chans), BF16)
@@ -331,31 +364,29 @@
     for size in factors(dp // 2):
         stages.append((stride, size))
         stride *= size
-    digits = [(rank // stride) % size for stride, size in stages]
-
-    x_edges = call(edge_kernel, [plane] * 2, [field], name="edges_x")
-    low_x, high_x = from_sides(*x_edges)
+    digits = [digit_of(stride, size) for stride, size in stages]
+
+    field = places.move(volume.reshape(planes, rows, chans))
+    grad_out = places.move(cotangent.reshape(planes, rows, chans))
     back_one, back_two = call(
-        turn_kernel,
-        [jax.ShapeDtypeStruct(w_one.shape, BF16)] * 2,
-        [w_one, w_two],
-        order=x_edges,
-        name="turn",
-    )
-    g_edges = call(edge_kernel, [plane] * 2, [grad_out], order=[back_two], name="edges_g")
-    low_g, high_g = from_sides(*g_edges)
-    wide_x, act, act_first, act_last, slope = call(
+        turn_kernel, [jax.ShapeDtypeStruct(w_one.shape, BF16)] * 2, [w_one, w_two], name="turn"
+    )
+    near_x, far_x = places.sides(*call(edge_kernel, [plane] * 2, [field], [odd], [back_two], name="edges_x"))
+    near_g, far_g = places.sides(*call(edge_kernel, [plane] * 2, [grad_out], [odd], name="edges_g"))
+    wide_x, act, *a_ends, slope = call(
         functools.partial(silu_kernel, side),
         [wide, slab, plane, plane, jax.ShapeDtypeStruct(slab.shape, F32)],
-        [field, low_x, high_x, w_one],
+        [field, near_x, far_x, w_one],
+        [odd],
         flops=flops,
         name="conv_pre",
     )
-    low_a, high_a = from_sides(act_first, act_last)
+    near_a, far_a = places.sides(*a_ends)
     wide_g, grad_pre = call(
         functools.partial(slope_kernel, side),
         [wide, slab],
-        [grad_out, low_g, high_g, back_two, slope],
+        [grad_out, near_g, far_g, back_two, slope],
+        [odd],
         flops=flops,
         name="conv_act_grad",
     )
@@ -363,9 +394,9 @@
     def outer(turned, own, spread_out, order, name):
         return call(
             functools.partial(outer_kernel, turned),
-            [tiles(half, chans, F32)] * 2,
+            [tiles(half, chans, F32)] * 2 + [plane] * (2 if turned else 0),
             [own, spread_out],
-            scalars=[core],
+            scalars=[core, odd],
             order=order,
             scratch=[
                 pltpu.VMEM((planes * chans, rows), BF16),
@@ -376,27 +407,30 @@
             name=name,
         )
 
-    keep_two, send_two = outer(False, act, wide_g, [], "outer_two")
+    keep_two, send_two = outer(False, act, wide_g, [near_a, far_a], "outer_two")
     got_two = swap_to(send_two, space, 2, 1, devices)
-    keep_one, send_one = outer(True, grad_pre, wide_x, [send_two], "outer_one")
+    keep_one, send_one, *d_ends = outer(True, grad_pre, wide_x, [send_two], "outer_one")
     got_one = swap_to(send_one, space, 2, 1, devices)
+    near_d, far_d = places.sides(*d_ends)
 
     def conv_out(order):
         return call(
             functools.partial(add_kernel, side),
             [slab],
-            [act, low_a, high_a, w_two, field],
+            [act, near_a, far_a, w_two, field],
+            [odd],
             order=order,
             scratch=[pltpu.VMEM(wide.shape, BF16)],
             flops=flops,
             name="conv_out",
         )[0]
 
-    def conv_in(order, low_d, high_d):
+    def conv_in(order):
         return call(
             functools.partial(add_kernel, side),
             [slab],
-            [grad_pre, low_d, high_d, back_one, grad_out],
+            [grad_pre, near_d, far_d, back_one, grad_out],
+            [odd],
             order=order,
             scratch=[pltpu.VMEM(wide.shape, BF16)],
             flops=flops,
@@ -414,34 +448,32 @@
         name="join",
     )
     got = [swap_to(s, stride, size, i + 1, devices) for i, s in enumerate(sends)]
-    order = [conv_out([kept])]
-    block_out = order[0]
-    d_edges = None
+    moved = [conv_out([kept])]
     for (stride, size), digit in zip(stages[1:], digits[1:]):
         piece = kept.shape[0] // size
-        carried = [] if d_edges else [grad_pre[:1], grad_pre[planes - 1 :]]
         outs = call(
-            functools.partial(scatter_kernel, size, len(got), len(carried)),
-            [tiles(piece, chans, F32)] + [tiles(piece, chans, BF16)] * (size - 1) + [plane] * len(carried),
-            [kept, *got, *carried],
+            functools.partial(scatter_kernel, size, len(got), len(moved)),
+            [tiles(piece, chans, F32)] + [tiles(piece, chans, BF16)] * (size - 1) + [slab] * len(moved),
+            [kept, *got, *moved],
             scalars=[digit],
-            order=order,
             name="scatter",
         )
         kept, sends = outs[0], outs[1:size]
         got = [swap_to(s, stride, size, i + 1, devices) for i, s in enumerate(sends)]
-        if carried:
-            d_edges = from_sides(*outs[size:])
-        order = []
+        if moved:
+            block_out = places.move(outs[size])
+            moved = []
+    input_grad = conv_in([kept])
     (mine,) = call(
         functools.partial(scatter_kernel, 1, len(got), 0),
         [tiles(kept.shape[0], chans, BF16)],
         [kept, *got],
         scalars=[digits[0]],
+        order=[input_grad],
         name="sum",
     )
-    input_grad = conv_in([mine], *d_edges)
-    order = [input_grad]
+    input_grad = places.move(input_grad)
+    order = []
     for (stride, size), digit in list(zip(stages, digits))[:0:-1]:
         pieces = [mine] + [swap_to(mine, stride, size, o, devices) for o in range(1, size)]
         (mine,) = call(

time: 111 us -> 95.4 us (0.86)
  Pallas kernels: 32.7 us -> 23.4 us
  starting transfers between devices: 44.3 us -> 40.8 us
  local copies, waits for them, and re-layouts: 6.89 us -> 3.93 us
    ppermute x18, waiting for transfers between devices: 13.7 us -> 25.9 us  [swap_to(): lax.ppermute(value, AXES, [(rank, partner(rank)) for rank in range(device...]
    ppermute x8 -> x12, waiting for transfers between devices: 12.2 us -> 0.03 us  [the longest x8 0.02 us: shift(): return lax.ppermute(value, AXES, pairs)]
    pallas_call x14, Pallas kernels: 32.7 us -> 23.4 us  [call(): pl.pallas_call(body, out_shape=list(outs), in_specs=[VMEM] * len(args) +...]
    ppermute x8 -> x12, starting transfers between devices: 23.6 us -> 20.1 us  [the longest x8 15.1 us: shift(): return lax.ppermute(value, AXES, pairs)]
    unnamed x36 -> x10, local copies, waits for them, and re-layouts: 6.86 us -> 3.93 us
  transfers between devices with their start and end apart: 26 -> 30, of which waited for: 9 -> 13; matrix products, arithmetic and copies ran while one was open for 0% -> 0% of each run, Pallas kernels for 17% -> 17%
where the time goes in v1:
time: 95.4 us; the launch traced here: 95 us
  starting transfers between devices  40.8 us (43%)
  waiting for transfers between devices  26 us (27%)
  Pallas kernels  23.4 us (25%)
  local copies, waits for them, and re-layouts  3.93 us (4%)
    ppermute x18, waiting for transfers between devices, swap_to(): lax.ppermute(value, AXES, [(rank, partner(rank)) for rank in range(device...  25.9 us
    pallas_call x14, Pallas kernels, call(): pl.pallas_call(body, out_shape=list(outs), in_specs=[VMEM] * len(args) +...  23.4 us
    ppermute x18, starting transfers between devices, swap_to(): lax.ppermute(value, AXES, [(rank, partner(rank)) for rank in range(device...  20.7 us
    ppermute x8, starting transfers between devices, shift(): return lax.ppermute(value, AXES, pairs)  15.1 us
    ppermute x4, starting transfers between devices, move(): return lax.ppermute(value, AXES, pairs)  4.96 us
    unnamed x10, local copies, waits for them, and re-layouts  3.93 us
  transfers between devices with their start and end apart: 30, of which 13 were waited for; matrix products, arithmetic and copies ran while one was open for 0% of the time, Pallas kernels for 17%

profile of v1, /device:TPU:0, one launch (start us, length us, event | category | flops | bytes accessed | tf_op | source)
XLA Modules:
  0.0 95.0 jit_solution(13664881063444298814)
XLA Ops:
  0.6 1.7 %collective-permute-start = (bf16[2,1024,128]{2,1,0:T(8,128)(2,1)}, bf16[2,1024,128]{2,1,0:T(8,128)(2,1)S(1)}, u32[]{:S(2)}, u32[]{:S(2)}) collective-permute-start(bf16[2,1024,128]{2,1,0:T(8,128)(2,1)} %bitcast.16), channel_id=1, source_target_pairs={{0,0},{1,4},{2,2},{3,6},{4,1},{5,5},{6,3},{7,7},{8,8},{9,12},{10,1... | collective-permute-start | bytes 1572872 | tf_op jit(solution)/shard_map/ppermute | solution.py:319
  2.3 1.7 %collective-permute-start.3 = (bf16[2,1024,128]{2,1,0:T(8,128)(2,1)}, bf16[2,1024,128]{2,1,0:T(8,128)(2,1)S(1)}, u32[]{:S(2)}, u32[]{:S(2)}) collective-permute-start(bf16[2,1024,128]{2,1,0:T(8,128)(2,1)} %bitcast.17), channel_id=1, source_target_pairs={{0,0},{1,4},{2,2},{3,6},{4,1},{5,5},{6,3},{7,7},{8,8},{9,12},{10,1... | collective-permute-start | bytes 1572872 | tf_op jit(solution)/shard_map/ppermute | solution.py:319
  6.4 2.0 %turn.1 = (bf16[3456,128]{1,0:T(8,128)(2,1)S(1)}, bf16[3456,128]{1,0:T(8,128)(2,1)S(1)}) custom-call(bf16[3456,128]{1,0:T(8,128)(2,1)S(1)} %bitcast.8, bf16[3456,128]{1,0:T(8,128)(2,1)S(1)} %bitcast.10), custom_call_target="tpu_custom_call" | custom-call | bytes 3538944 | tf_op jit(solution)/shard_map/turn/pallas_call | solution.py:47
  8.4 4.4 %collective-permute-start.1 = (bf16[1,1024,128]{2,1,0:T(8,128)(2,1)S(1)}, bf16[1,1024,128]{2,1,0:T(8,128)(2,1)S(1)}, u32[]{:S(2)}, u32[]{:S(2)}) collective-permute-start(bf16[1,1024,128]{2,1,0:T(8,128)(2,1)S(1)} %get-tuple-element.35), channel_id=1, source_target_pairs={{0,4},{4,0},{2,6},{6,2},{1,5},{5,1},{3,7},{7,3},{8,12},{12,8},{10,... | collective-permute-start | bytes 786440 | tf_op jit(solution)/shard_map/ppermute | solution.py:328
  13.5 4.9 %collective-permute-start.4 = (bf16[1,1024,128]{2,1,0:T(8,128)(2,1)S(1)}, bf16[1,1024,128]{2,1,0:T(8,128)(2,1)S(1)}, u32[]{:S(2)}, u32[]{:S(2)}) collective-permute-start(bf16[1,1024,128]{2,1,0:T(8,128)(2,1)S(1)} %get-tuple-element.38), channel_id=1, source_target_pairs={{0,4},{4,0},{2,6},{6,2},{1,5},{5,1},{3,7},{7,3},{8,12},{12,8},{10,... | collective-permute-start | bytes 786440 | tf_op jit(solution)/shard_map/ppermute | solution.py:328
  19.1 3.6 %conv_pre.1 = (bf16[4,1088,384]{2,1,0:T(8,128)(2,1)S(1)}, bf16[2,1024,128]{2,1,0:T(8,128)(2,1)S(1)}, bf16[1,1024,128]{2,1,0:T(8,128)(2,1)S(1)}, bf16[1,1024,128]{2,1,0:T(8,128)(2,1)S(1)}, f32[2,1024,128]{2,1,0:T(8,128)S(1)}) custom-call(bf16[2,1024,128]{2,1,0:T(8,128)(2,1)S(1)} %collective-permute-done.refs_0_.refs_4_, ...), custom_call_target="tpu_custom_call" | custom-call | flops 1811939328 | bytes 7372800 | tf_op jit(solution)/shard_map/conv_pre/pallas_call | solution.py:47
  22.7 3.2 %collective-permute-start.6 = (bf16[1,1024,128]{2,1,0:T(8,128)(2,1)S(1)}, bf16[1,1024,128]{2,1,0:T(8,128)(2,1)S(1)}, u32[]{:S(2)}, u32[]{:S(2)}) collective-permute-start(bf16[1,1024,128]{2,1,0:T(8,128)(2,1)S(1)} %get-tuple-element.42), channel_id=1, source_target_pairs={{0,4},{4,0},{2,6},{6,2},{1,5},{5,1},{3,7},{7,3},{8,12},{12,8},{10,... | collective-permute-start | bytes 786440 | tf_op jit(solution)/shard_map/ppermute | solution.py:328
  26.6 3.4 %conv_act_grad.1 = (bf16[4,1088,384]{2,1,0:T(8,128)(2,1)S(1)}, bf16[2,1024,128]{2,1,0:T(8,128)(2,1)S(1)}) custom-call(bf16[2,1024,128]{2,1,0:T(8,128)(2,1)S(1)} %collective-permute-done.3.refs_0_.refs_4_, bf16[1,1024,128]{2,1,0:T(8,128)(2,1)S(1)} %collective-permute-done.4.refs_1_, bf16[1,1024,128]{2,1,0:T(8,128)(2,1)S(1)} %collective-permute-done.5.refs_2_, ...), custom_call_target="tpu_custom_call" | custom-call | flops 1811939328 | bytes 6848512 | tf_op jit(solution)/shard_map/conv_act_grad/pallas_call | solution.py:47
  30.1 2.4 %outer_two.1 = (f32[216,8,128]{2,1,0:T(8,128)S(1)}, f32[216,8,128]{2,1,0:T(8,128)S(1)}) custom-call(bf16[2,1024,128]{2,1,0:T(8,128)(2,1)S(1)} %get-tuple-element.37.refs_0_, bf16[4,1088,384]{2,1,0:T(8,128)(2,1)S(1)} %get-tuple-element.41.refs_1_, bf16[1,1024,128]{2,1,0:T(8,128)(2,1)S(1)} %collective-permute-done.6.refs_2_.refs_1_, ...), custom_call_target="tpu_custom_call" | custom-call | flops 1811939328 | bytes 5636096 | tf_op jit(solution)/shard_map/outer_two/pallas_call | solution.py:47
  32.5 2.5 %outer_one.1 = (f32[216,8,128]{2,1,0:T(8,128)S(1)}, f32[216,8,128]{2,1,0:T(8,128)S(1)}, bf16[1,1024,128]{2,1,0:T(8,128)(2,1)S(1)}, bf16[1,1024,128]{2,1,0:T(8,128)(2,1)S(1)}) custom-call(bf16[2,1024,128]{2,1,0:T(8,128)(2,1)S(1)} %get-tuple-element.46.refs_0_, bf16[4,1088,384]{2,1,0:T(8,128)(2,1)S(1)} %get-tuple-element.47.refs_1_, ...), custom_call_target="tpu_custom_call" | custom-call | flops 1811939328 | bytes 6160384 | tf_op jit(solution)/shard_map/outer_one/pallas_call | solution.py:47
  35.0 3.7 %collective-permute-start.9 = (f32[216,8,128]{2,1,0:T(8,128)S(1)}, f32[216,8,128]{2,1,0:T(8,128)S(1)}, u32[]{:S(2)}, u32[]{:S(2)}) collective-permute-start(f32[216,8,128]{2,1,0:T(8,128)S(1)} %get-tuple-element.49), channel_id=1, source_target_pairs={{0,4},{1,5},{2,6},{3,7},{4,0},{5,1},{6,2},{7,3},{8,12},{9,13},{10,... | collective-permute-start | bytes 2654216 | tf_op jit(solution)/shard_map/ppermute | solution.py:36
  38.8 2.0 %collective-permute-done.9.refs_3_ = f32[216,8,128]{2,1,0:T(8,128)S(1)} collective-permute-done((f32[216,8,128]{2,1,0:T(8,128)S(1)}, f32[216,8,128]{2,1,0:T(8,128)S(1)}, u32[]{:S(2)}, u32[]{:S(2)}) %collective-permute-start.9) | collective-permute-done | bytes 884768 | tf_op jit(solution)/shard_map/ppermute | solution.py:36
  46.5 3.4 %conv_out.1.refs_4_ = bf16[2,1024,128]{2,1,0:T(8,128)(2,1)S(1)} custom-call(bf16[2,1024,128]{2,1,0:T(8,128)(2,1)S(1)} %get-tuple-element.37.refs_0_, bf16[1,1024,128]{2,1,0:T(8,128)(2,1)S(1)} %collective-permute-done.6.refs_2_.refs_1_, bf16[1,1024,128]{2,1,0:T(8,128)(2,1)S(1)} %collective-permute-done.7.refs_3_.refs_2_, bf16[3456,128]{1,0:T(8,128)(2,1)S(1)} %bitcast.11, ...), custom_call_target="tpu_custom_call" | custom-call | flops 1811939328 | bytes 2981888 | tf_op jit(solution)/shard_map/conv_out/pallas_call | solution.py:47
  50.6 5.2 %collective-permute-done.11.refs_2_ = bf16[108,8,128]{2,1,0:T(8,128)(2,1)S(1)} collective-permute-done((bf16[108,8,128]{2,1,0:T(8,128)(2,1)S(1)}, bf16[108,8,128]{2,1,0:T(8,128)(2,1)S(1)}, u32[]{:S(2)}, u32[]{:S(2)}) %collective-permute-start.11) | collective-permute-done | bytes 221216 | tf_op jit(solution)/shard_map/ppermute | solution.py:36
  58.5 2.6 %collective-permute-start.18 = (bf16[27,8,128]{2,1,0:T(8,128)(2,1)S(1)}, bf16[27,8,128]{2,1,0:T(8,128)(2,1)S(1)}, u32[]{:S(2)}, u32[]{:S(2)}) collective-permute-start(bf16[27,8,128]{2,1,0:T(8,128)(2,1)S(1)} %get-tuple-element.60), channel_id=1, source_target_pairs={{0,16},{1,17},{2,18},{3,19},{4,20},{5,21},{6,22},{7,23},{8,24},{9,... | collective-permute-start | bytes 165896 | tf_op jit(solution)/shard_map/ppermute | solution.py:36
  61.3 3.4 %conv_in.1.refs_4_ = bf16[2,1024,128]{2,1,0:T(8,128)(2,1)S(1)} custom-call(bf16[2,1024,128]{2,1,0:T(8,128)(2,1)S(1)} %get-tuple-element.46.refs_0_, bf16[1,1024,128]{2,1,0:T(8,128)(2,1)S(1)} %collective-permute-done.14.refs_1_, bf16[1,1024,128]{2,1,0:T(8,128)(2,1)S(1)} %collective-permute-done.15.refs_2_, bf16[3456,128]{1,0:T(8,128)(2,1)S(1)} %get-tuple-element.57.refs_3_, ...), custom_call_target="tpu_custom_call" | custom-call | flops 1811939328 | bytes 2981888 | tf_op jit(solution)/shard_map/conv_in/pallas_call | solution.py:47
  65.4 1.8 %collective-permute-done.19.refs_3_ = bf16[27,8,128]{2,1,0:T(8,128)(2,1)S(1)} collective-permute-done((bf16[27,8,128]{2,1,0:T(8,128)(2,1)S(1)}, bf16[27,8,128]{2,1,0:T(8,128)(2,1)S(1)}, u32[]{:S(2)}, u32[]{:S(2)}) %collective-permute-start.19) | collective-permute-done | bytes 55328 | tf_op jit(solution)/shard_map/ppermute | solution.py:36
  67.3 1.9 %collective-permute-start.22 = (bf16[27,8,128]{2,1,0:T(8,128)(2,1)S(1)}, bf16[27,8,128]{2,1,0:T(8,128)(2,1)S(1)}, u32[]{:S(2)}, u32[]{:S(2)}) collective-permute-start(bf16[27,8,128]{2,1,0:T(8,128)(2,1)S(1)} %sum.1.refs_0_), channel_id=1, source_target_pairs={{0,24},{1,25},{2,26},{3,27},{4,28},{5,29},{6,30},{7,31},{8,16},{9,... | collective-permute-start | bytes 165896 | tf_op jit(solution)/shard_map/ppermute | solution.py:36
  69.1 2.6 %collective-permute-start.20 = (bf16[27,8,128]{2,1,0:T(8,128)(2,1)S(1)}, bf16[27,8,128]{2,1,0:T(8,128)(2,1)S(1)}, u32[]{:S(2)}, u32[]{:S(2)}) collective-permute-start(bf16[27,8,128]{2,1,0:T(8,128)(2,1)S(1)} %sum.1.refs_0_), channel_id=1, source_target_pairs={{0,8},{1,9},{2,10},{3,11},{4,12},{5,13},{6,14},{7,15},{8,0},{9,1},... | collective-permute-start | bytes 165896 | tf_op jit(solution)/shard_map/ppermute | solution.py:36
  73.3 2.5 %collective-permute-done.21.refs_2_ = bf16[27,8,128]{2,1,0:T(8,128)(2,1)S(1)} collective-permute-done((bf16[27,8,128]{2,1,0:T(8,128)(2,1)S(1)}, bf16[27,8,128]{2,1,0:T(8,128)(2,1)S(1)}, u32[]{:S(2)}, u32[]{:S(2)}) %collective-permute-start.21) | collective-permute-done | bytes 55328 | tf_op jit(solution)/shard_map/ppermute | solution.py:36
  75.8 3.1 %collective-permute-start.25 = (bf16[108,8,128]{2,1,0:T(8,128)(2,1)S(1)}, bf16[108,8,128]{2,1,0:T(8,128)(2,1)S(1)}, u32[]{:S(2)}, u32[]{:S(2)}) collective-permute-start(bf16[108,8,128]{2,1,0:T(8,128)(2,1)S(1)} %gather.1.refs_0_), channel_id=1, source_target_pairs={{0,3},{1,2},{2,1},{3,0},{4,7},{5,6},{6,5},{7,4},{8,11},{9,10},{10,... | collective-permute-start | bytes 663560 | tf_op jit(solution)/shard_map/ppermute | solution.py:36
  79.8 5.5 %collective-permute-done.25.refs_3_ = bf16[108,8,128]{2,1,0:T(8,128)(2,1)S(1)} collective-permute-done((bf16[108,8,128]{2,1,0:T(8,128)(2,1)S(1)}, bf16[108,8,128]{2,1,0:T(8,128)(2,1)S(1)}, u32[]{:S(2)}, u32[]{:S(2)}) %collective-permute-start.25) | collective-permute-done | bytes 221216 | tf_op jit(solution)/shard_map/ppermute | solution.py:36
  85.3 3.4 %collective-permute-done.24.refs_2_ = bf16[108,8,128]{2,1,0:T(8,128)(2,1)S(1)} collective-permute-done((bf16[108,8,128]{2,1,0:T(8,128)(2,1)S(1)}, bf16[108,8,128]{2,1,0:T(8,128)(2,1)S(1)}, u32[]{:S(2)}, u32[]{:S(2)}) %collective-permute-start.24) | collective-permute-done | bytes 221216 | tf_op jit(solution)/shard_map/ppermute | solution.py:36
  91.2 2.2 %finish.1 = (f32[432,8,128]{2,1,0:T(8,128)}, f32[432,8,128]{2,1,0:T(8,128)}) custom-call(bf16[108,8,128]{2,1,0:T(8,128)(2,1)S(1)} %gather.1.refs_0_, bf16[108,8,128]{2,1,0:T(8,128)(2,1)S(1)} %collective-permute-done.23.refs_1_, bf16[108,8,128]{2,1,0:T(8,128)(2,1)S(1)} %collective-permute-done.24.refs_2_, ...), custom_call_target="tpu_custom_call" | custom-call | bytes 5308416 | tf_op jit(solution)/shard_map/finish/pallas_call | solution.py:47
  (60 shorter events, 21.2 us)
Async XLA Ops:
  0.6 7.7 %collective-permute-start = (bf16[2,1024,128]{2,1,0:T(8,128)(2,1)}, bf16[2,1024,128]{2,1,0:T(8,128)(2,1)S(1)}, u32[]{:S(2)}, u32[]{:S(2)}) collective-permute-start(bf16[2,1024,128]{2,1,0:T(8,128)(2,1)} %bitcast.16), channel_id=1, source_target_pairs={{0,0},{1,4},{2,2},{3,6},{4,1},{5,5},{6,3},{7,7},{8,8},{9,12},{10,1... | collective-permute-start | bytes 1572872 | tf_op jit(solution)/shard_map/ppermute | solution.py:319
  2.3 11.1 %collective-permute-start.3 = (bf16[2,1024,128]{2,1,0:T(8,128)(2,1)}, bf16[2,1024,128]{2,1,0:T(8,128)(2,1)S(1)}, u32[]{:S(2)}, u32[]{:S(2)}) collective-permute-start(bf16[2,1024,128]{2,1,0:T(8,128)(2,1)} %bitcast.17), channel_id=1, source_target_pairs={{0,0},{1,4},{2,2},{3,6},{4,1},{5,5},{6,3},{7,7},{8,8},{9,12},{10,1... | collective-permute-start | bytes 1572872 | tf_op jit(solution)/shard_map/ppermute | solution.py:319
  8.4 10.7 %collective-permute-start.1 = (bf16[1,1024,128]{2,1,0:T(8,128)(2,1)S(1)}, bf16[1,1024,128]{2,1,0:T(8,128)(2,1)S(1)}, u32[]{:S(2)}, u32[]{:S(2)}) collective-permute-start(bf16[1,1024,128]{2,1,0:T(8,128)(2,1)S(1)} %get-tuple-element.35), channel_id=1, source_target_pairs={{0,4},{4,0},{2,6},{6,2},{1,5},{5,1},{3,7},{7,3},{8,12},{12,8},{10,... | collective-permute-start | bytes 786440 | tf_op jit(solution)/shard_map/ppermute | solution.py:328
  12.8 6.3 %collective-permute-start.2 = (bf16[1,1024,128]{2,1,0:T(8,128)(2,1)S(1)}, bf16[1,1024,128]{2,1,0:T(8,128)(2,1)S(1)}, u32[]{:S(2)}, u32[]{:S(2)}) collective-permute-start(bf16[1,1024,128]{2,1,0:T(8,128)(2,1)S(1)} %get-tuple-element.36), channel_id=1, source_target_pairs={{4,2},{2,4},{5,3},{3,5},{12,10},{10,12},{13,11},{11,13},{20,18},{1... | collective-permute-start | bytes 786440 | tf_op jit(solution)/shard_map/ppermute | solution.py:328
  13.5 13.1 %collective-permute-start.4 = (bf16[1,1024,128]{2,1,0:T(8,128)(2,1)S(1)}, bf16[1,1024,128]{2,1,0:T(8,128)(2,1)S(1)}, u32[]{:S(2)}, u32[]{:S(2)}) collective-permute-start(bf16[1,1024,128]{2,1,0:T(8,128)(2,1)S(1)} %get-tuple-element.38), channel_id=1, source_target_pairs={{0,4},{4,0},{2,6},{6,2},{1,5},{5,1},{3,7},{7,3},{8,12},{12,8},{10,... | collective-permute-start | bytes 786440 | tf_op jit(solution)/shard_map/ppermute | solution.py:328
  18.4 8.2 %collective-permute-start.5 = (bf16[1,1024,128]{2,1,0:T(8,128)(2,1)S(1)}, bf16[1,1024,128]{2,1,0:T(8,128)(2,1)S(1)}, u32[]{:S(2)}, u32[]{:S(2)}) collective-permute-start(bf16[1,1024,128]{2,1,0:T(8,128)(2,1)S(1)} %get-tuple-element.39), channel_id=1, source_target_pairs={{4,2},{2,4},{5,3},{3,5},{12,10},{10,12},{13,11},{11,13},{20,18},{1... | collective-permute-start | bytes 786440 | tf_op jit(solution)/shard_map/ppermute | solution.py:328
  22.7 7.3 %collective-permute-start.6 = (bf16[1,1024,128]{2,1,0:T(8,128)(2,1)S(1)}, bf16[1,1024,128]{2,1,0:T(8,128)(2,1)S(1)}, u32[]{:S(2)}, u32[]{:S(2)}) collective-permute-start(bf16[1,1024,128]{2,1,0:T(8,128)(2,1)S(1)} %get-tuple-element.42), channel_id=1, source_target_pairs={{0,4},{4,0},{2,6},{6,2},{1,5},{5,1},{3,7},{7,3},{8,12},{12,8},{10,... | collective-permute-start | bytes 786440 | tf_op jit(solution)/shard_map/ppermute | solution.py:328
  35.0 5.7 %collective-permute-start.9 = (f32[216,8,128]{2,1,0:T(8,128)S(1)}, f32[216,8,128]{2,1,0:T(8,128)S(1)}, u32[]{:S(2)}, u32[]{:S(2)}) collective-permute-start(f32[216,8,128]{2,1,0:T(8,128)S(1)} %get-tuple-element.49), channel_id=1, source_target_pairs={{0,4},{1,5},{2,6},{3,7},{4,0},{5,1},{6,2},{7,3},{8,12},{9,13},{10,... | collective-permute-start | bytes 2654216 | tf_op jit(solution)/shard_map/ppermute | solution.py:36
  42.2 8.4 %collective-permute-start.10 = (bf16[108,8,128]{2,1,0:T(8,128)(2,1)S(1)}, bf16[108,8,128]{2,1,0:T(8,128)(2,1)S(1)}, u32[]{:S(2)}, u32[]{:S(2)}) collective-permute-start(bf16[108,8,128]{2,1,0:T(8,128)(2,1)S(1)} %get-tuple-element.51), channel_id=1, source_target_pairs={{0,1},{1,0},{2,3},{3,2},{4,5},{5,4},{6,7},{7,6},{8,9},{9,8},{10,11... | collective-permute-start | bytes 663560 | tf_op jit(solution)/shard_map/ppermute | solution.py:36
  43.7 12.2 %collective-permute-start.11 = (bf16[108,8,128]{2,1,0:T(8,128)(2,1)S(1)}, bf16[108,8,128]{2,1,0:T(8,128)(2,1)S(1)}, u32[]{:S(2)}, u32[]{:S(2)}) collective-permute-start(bf16[108,8,128]{2,1,0:T(8,128)(2,1)S(1)} %get-tuple-element.52), channel_id=1, source_target_pairs={{0,2},{1,3},{2,0},{3,1},{4,6},{5,7},{6,4},{7,5},{8,10},{9,11},{10,... | collective-permute-start | bytes 663560 | tf_op jit(solution)/shard_map/ppermute | solution.py:36
  44.5 11.3 %collective-permute-start.12 = (bf16[108,8,128]{2,1,0:T(8,128)(2,1)S(1)}, bf16[108,8,128]{2,1,0:T(8,128)(2,1)S(1)}, u32[]{:S(2)}, u32[]{:S(2)}) collective-permute-start(bf16[108,8,128]{2,1,0:T(8,128)(2,1)S(1)} %get-tuple-element.53), channel_id=1, source_target_pairs={{0,3},{1,2},{2,1},{3,0},{4,7},{5,6},{6,5},{7,4},{8,11},{9,10},{10,... | collective-permute-start | bytes 663560 | tf_op jit(solution)/shard_map/ppermute | solution.py:36
  45.8 15.3 %collective-permute-start.14 = (bf16[1,1024,128]{2,1,0:T(8,128)(2,1)S(1)}, bf16[1,1024,128]{2,1,0:T(8,128)(2,1)S(1)}, u32[]{:S(2)}, u32[]{:S(2)}) collective-permute-start(bf16[1,1024,128]{2,1,0:T(8,128)(2,1)S(1)} %get-tuple-element.55), channel_id=1, source_target_pairs={{0,4},{4,0},{2,6},{6,2},{1,5},{5,1},{3,7},{7,3},{8,12},{12,8},{10,... | collective-permute-start | bytes 786440 | tf_op jit(solution)/shard_map/ppermute | solution.py:328
  45.8 15.5 %collective-permute-start.15 = (bf16[1,1024,128]{2,1,0:T(8,128)(2,1)S(1)}, bf16[1,1024,128]{2,1,0:T(8,128)(2,1)S(1)}, u32[]{:S(2)}, u32[]{:S(2)}) collective-permute-start(bf16[1,1024,128]{2,1,0:T(8,128)(2,1)S(1)} %get-tuple-element.56), channel_id=1, source_target_pairs={{4,2},{2,4},{5,3},{3,5},{12,10},{10,12},{13,11},{11,13},{20,18},{1... | collective-permute-start | bytes 786440 | tf_op jit(solution)/shard_map/ppermute | solution.py:328
  56.0 33.4 %collective-permute-start.13 = (bf16[2,1024,128]{2,1,0:T(8,128)(2,1)S(1)}, bf16[2,1024,128]{2,1,0:T(8,128)(2,1)S(1)}, u32[]{:S(2)}, u32[]{:S(2)}) collective-permute-start(bf16[2,1024,128]{2,1,0:T(8,128)(2,1)S(1)} %get-tuple-element.54), channel_id=1, source_target_pairs={{0,0},{1,4},{2,2},{3,6},{4,1},{5,5},{6,3},{7,7},{8,8},{9,12},{10,1... | collective-permute-start | bytes 1572872 | tf_op jit(solution)/shard_map/ppermute | solution.py:319
  56.9 8.5 %collective-permute-start.17 = (bf16[27,8,128]{2,1,0:T(8,128)(2,1)S(1)}, bf16[27,8,128]{2,1,0:T(8,128)(2,1)S(1)}, u32[]{:S(2)}, u32[]{:S(2)}) collective-permute-start(bf16[27,8,128]{2,1,0:T(8,128)(2,1)S(1)} %get-tuple-element.59), channel_id=1, source_target_pairs={{0,8},{1,9},{2,10},{3,11},{4,12},{5,13},{6,14},{7,15},{8,0},{9,1},... | collective-permute-start | bytes 165896 | tf_op jit(solution)/shard_map/ppermute | solution.py:36
  58.5 6.9 %collective-permute-start.18 = (bf16[27,8,128]{2,1,0:T(8,128)(2,1)S(1)}, bf16[27,8,128]{2,1,0:T(8,128)(2,1)S(1)}, u32[]{:S(2)}, u32[]{:S(2)}) collective-permute-start(bf16[27,8,128]{2,1,0:T(8,128)(2,1)S(1)} %get-tuple-element.60), channel_id=1, source_target_pairs={{0,16},{1,17},{2,18},{3,19},{4,20},{5,21},{6,22},{7,23},{8,24},{9,... | collective-permute-start | bytes 165896 | tf_op jit(solution)/shard_map/ppermute | solution.py:36
  61.1 6.1 %collective-permute-start.19 = (bf16[27,8,128]{2,1,0:T(8,128)(2,1)S(1)}, bf16[27,8,128]{2,1,0:T(8,128)(2,1)S(1)}, u32[]{:S(2)}, u32[]{:S(2)}) collective-permute-start(bf16[27,8,128]{2,1,0:T(8,128)(2,1)S(1)} %get-tuple-element.61), channel_id=1, source_target_pairs={{0,24},{1,25},{2,26},{3,27},{4,28},{5,29},{6,30},{7,31},{8,16},{9,... | collective-permute-start | bytes 165896 | tf_op jit(solution)/shard_map/ppermute | solution.py:36
  64.7 25.2 %collective-permute-start.16 = (bf16[2,1024,128]{2,1,0:T(8,128)(2,1)S(1)}, bf16[2,1024,128]{2,1,0:T(8,128)(2,1)S(1)}, u32[]{:S(2)}, u32[]{:S(2)}) collective-permute-start(bf16[2,1024,128]{2,1,0:T(8,128)(2,1)S(1)} %conv_in.1.refs_4_), channel_id=1, source_target_pairs={{0,0},{1,4},{2,2},{3,6},{4,1},{5,5},{6,3},{7,7},{8,8},{9,12},{10,1... | collective-permute-start | bytes 1572872 | tf_op jit(solution)/shard_map/ppermute | solution.py:319
  67.3 6.0 %collective-permute-start.22 = (bf16[27,8,128]{2,1,0:T(8,128)(2,1)S(1)}, bf16[27,8,128]{2,1,0:T(8,128)(2,1)S(1)}, u32[]{:S(2)}, u32[]{:S(2)}) collective-permute-start(bf16[27,8,128]{2,1,0:T(8,128)(2,1)S(1)} %sum.1.refs_0_), channel_id=1, source_target_pairs={{0,24},{1,25},{2,26},{3,27},{4,28},{5,29},{6,30},{7,31},{8,16},{9,... | collective-permute-start | bytes 165896 | tf_op jit(solution)/shard_map/ppermute | solution.py:36
  69.1 6.6 %collective-permute-start.21 = (bf16[27,8,128]{2,1,0:T(8,128)(2,1)S(1)}, bf16[27,8,128]{2,1,0:T(8,128)(2,1)S(1)}, u32[]{:S(2)}, u32[]{:S(2)}) collective-permute-start(bf16[27,8,128]{2,1,0:T(8,128)(2,1)S(1)} %sum.1.refs_0_), channel_id=1, source_target_pairs={{0,16},{1,17},{2,18},{3,19},{4,20},{5,21},{6,22},{7,23},{8,24},{9,... | collective-permute-start | bytes 165896 | tf_op jit(solution)/shard_map/ppermute | solution.py:36
  69.1 6.6 %collective-permute-start.20 = (bf16[27,8,128]{2,1,0:T(8,128)(2,1)S(1)}, bf16[27,8,128]{2,1,0:T(8,128)(2,1)S(1)}, u32[]{:S(2)}, u32[]{:S(2)}) collective-permute-start(bf16[27,8,128]{2,1,0:T(8,128)(2,1)S(1)} %sum.1.refs_0_), channel_id=1, source_target_pairs={{0,8},{1,9},{2,10},{3,11},{4,12},{5,13},{6,14},{7,15},{8,0},{9,1},... | collective-permute-start | bytes 165896 | tf_op jit(solution)/shard_map/ppermute | solution.py:36
  75.8 9.4 %collective-permute-start.25 = (bf16[108,8,128]{2,1,0:T(8,128)(2,1)S(1)}, bf16[108,8,128]{2,1,0:T(8,128)(2,1)S(1)}, u32[]{:S(2)}, u32[]{:S(2)}) collective-permute-start(bf16[108,8,128]{2,1,0:T(8,128)(2,1)S(1)} %gather.1.refs_0_), channel_id=1, source_target_pairs={{0,3},{1,2},{2,1},{3,0},{4,7},{5,6},{6,5},{7,4},{8,11},{9,10},{10,... | collective-permute-start | bytes 663560 | tf_op jit(solution)/shard_map/ppermute | solution.py:36
  78.9 9.7 %collective-permute-start.24 = (bf16[108,8,128]{2,1,0:T(8,128)(2,1)S(1)}, bf16[108,8,128]{2,1,0:T(8,128)(2,1)S(1)}, u32[]{:S(2)}, u32[]{:S(2)}) collective-permute-start(bf16[108,8,128]{2,1,0:T(8,128)(2,1)S(1)} %gather.1.refs_0_), channel_id=1, source_target_pairs={{0,2},{1,3},{2,0},{3,1},{4,6},{5,7},{6,4},{7,5},{8,10},{9,11},{10,... | collective-permute-start | bytes 663560 | tf_op jit(solution)/shard_map/ppermute | solution.py:36
  79.8 9.6 %collective-permute-start.23 = (bf16[108,8,128]{2,1,0:T(8,128)(2,1)S(1)}, bf16[108,8,128]{2,1,0:T(8,128)(2,1)S(1)}, u32[]{:S(2)}, u32[]{:S(2)}) collective-permute-start(bf16[108,8,128]{2,1,0:T(8,128)(2,1)S(1)} %gather.1.refs_0_), channel_id=1, source_target_pairs={{0,1},{1,0},{2,3},{3,2},{4,5},{5,4},{6,7},{7,6},{8,9},{9,8},{10,11... | collective-permute-start | bytes 663560 | tf_op jit(solution)/shard_map/ppermute | solution.py:36
  (10 other events, 43.4 us)
